TPU v7x, 32 devices: a whole 2x2x4 slice. The times are simulated.
32 devices in a mesh: blk: 8 (over z, core), seq: 4 (over y, x).
Axes of the slice: x: 2, y: 2, z: 4, core: 2. Of those that a mesh axis runs over, the one named last changes fastest.
Arguments:
- activations: bfloat16 [8, 2048, 8192], P('blk', 'seq'), may hold values from -6 to 6
- base_weight: bfloat16 [8192, 1024], P('blk', 'seq'), may hold values from -0.0625 to 0.0625
- adapter_down: bfloat16 [8, 16, 8192], P('blk'), may hold values from -0.0625 to 0.0625
- adapter_up: bfloat16 [8, 16, 1024], P('blk'), may hold values from -1.5 to 1.5
- cotangent: bfloat16 [8, 2048, 1024], P('blk', 'seq'), may hold values from -12 to 12
Outputs:
- projected: bfloat16 [8, 2048, 1024], P('blk', 'seq')
- gradient_inputs: bfloat16 [8, 2048, 8192], P('blk', 'seq')
- down_gradient: float32 [8, 16, 8192], P('blk')
- up_gradient: float32 [8, 16, 1024], P('blk')
All inputs are finite; a program needn't handle non-finite values.
Results may differ from a plain program's by a relative error of at most 0.0047.
Values may be sent and summed in bfloat16 or wider, within the bound.
No kernel may reach another device: no remote copies, remote signals or barrier semaphores. Data moves between devices by JAX's collectives and lax.ppermute only.
A program may use at most 128 MiB of HBM per device.

v0:
```python
import jax
import jax.numpy as jnp
from jax import lax
from jax.sharding import PartitionSpec as P

adapter_scale = 2.0


def body(activations, base_weight, adapter_down, adapter_up, cotangent):
    token_inputs = activations[0]
    down_matrix = adapter_down[0]
    up_matrix = adapter_up[0]
    output_cotangent = cotangent[0]
    token_count = token_inputs.shape[0] * lax.axis_size("seq")
    panel = lax.all_gather(base_weight, "seq", axis=1, tiled=True)
    lowrank_forward = jnp.dot(
        token_inputs, down_matrix.T, preferred_element_type=jnp.float32
    ).astype(jnp.bfloat16)
    lowrank_backward = jnp.dot(
        output_cotangent, up_matrix.T, preferred_element_type=jnp.float32
    ).astype(jnp.bfloat16)
    frozen_keys = jnp.dot(
        token_inputs,
        lax.all_gather(panel, "blk", axis=0, tiled=True),
        preferred_element_type=jnp.float32,
    )
    frozen_gradient = lax.dot_general(
        output_cotangent,
        lax.all_gather(panel, "blk", axis=0, tiled=True),
        (((1,), (1,)), ((), ())),
        preferred_element_type=jnp.float32,
    )
    projected = frozen_keys + adapter_scale * jnp.dot(
        lowrank_forward, up_matrix, preferred_element_type=jnp.float32
    )
    gradient_inputs = frozen_gradient + adapter_scale * jnp.dot(
        lowrank_backward, down_matrix, preferred_element_type=jnp.float32
    )
    local_down = jnp.dot(lowrank_backward.T, token_inputs, preferred_element_type=jnp.float32)
    local_up = jnp.dot(lowrank_forward.T, output_cotangent, preferred_element_type=jnp.float32)
    sum_down, sum_up = lax.psum((local_down, local_up), "seq")
    scale_factor = adapter_scale / token_count
    return (
        projected.astype(jnp.bfloat16)[None],
        gradient_inputs.astype(jnp.bfloat16)[None],
        (scale_factor * sum_down)[None],
        (scale_factor * sum_up)[None],
    )


def solution(mesh):
    return jax.shard_map(
        body,
        mesh=mesh,
        in_specs=(
            P("blk", "seq", None),
            P("blk", "seq"),
            P("blk", None, None),
            P("blk", None, None),
            P("blk", "seq", None),
        ),
        out_specs=(
            P("blk", "seq", None),
            P("blk", "seq", None),
            P("blk", None, None),
            P("blk", None, None),
        ),
        check_vma=False,
    )
```

profile of v0, /device:TPU:0, one launch (start us, length us, event | category | flops | bytes accessed | tf_op | source)
XLA Modules:
  0.0 299.8 jit_solution(208566958700023274)
XLA Ops:
  7.2 0.0 copy-start
  7.2 0.0 all-gather.3.cloned.1.call-start
  7.2 0.7 all-gather.3.cloned.1.call-update
  7.9 0.0 all-reduce.3.cloned.1.call-start
  8.0 0.4 copy-done
  8.4 0.0 copy-start.1
  8.4 1.3 convolution_convert_fusion
  9.7 6.0 %fusion.12 = bf16[512,16]{0,1:T(8,128)(2,1)S(1)} fusion(bf16[1,512,8192]{2,1,0:T(8,128)(2,1)} %param.5, bf16[1,16,8192]{2,1,0:T(8,128)(2,1)} %param.7), kind=kOutput, calls=%fused_computation.10 | convolution fusion | flops 134225920 | bytes 8667136 | tf_op jit(solution)/shard_map/dot_general | solution.py:16
  15.6 0.0 copy-start.3
  15.6 0.9 fusion.15
  16.5 0.0 copy-done.1
  16.6 2.0 fusion.1
  18.6 0.0 all-reduce.3.cloned.1.call-update
  18.6 0.2 all-gather.5.cloned.1.call-start
  18.8 28.9 %all-gather.3.cloned.1.call-done = bf16[1024,1024]{1,0:T(8,128)(2,1)} async-done(((bf16[1024,256]{1,0:T(8,128)(2,1)}), bf16[1024,1024]{1,0:T(8,128)(2,1)}) %all-gather.3.cloned.1.call-update) | async-done | bytes 2097168 | tf_op jit(solution)/shard_map/all_gather | solution.py:15
  47.7 0.0 all-gather.5.cloned.1.call-update
  47.8 0.0 copy-done.3
  47.8 0.5 fusion.23
  48.2 49.4 %all-reduce.3.cloned.1.call-done = (f32[16,8192]{1,0:T(8,128)}, f32[16,1024]{1,0:T(8,128)}) async-done(((f32[16,8192]{1,0:T(8,128)}, f32[16,1024]{1,0:T(8,128)}), (f32[16,8192]{1,0:T(8,128)}, f32[16,1024]{1,0:T(8,128)})) %all-reduce.3.cloned.1.call-update) | async-done | bytes 589840 | tf_op jit(solution)/shard_map/psum | solution.py:41
  97.6 1.5 multiply_bitcast_fusion.1
  99.1 1.9 multiply_bitcast_fusion
  100.9 0.0 copy-start.2
  100.9 149.5 %all-gather.5.cloned.1.call-done = bf16[8192,1024]{1,0:T(8,128)(2,1)} async-done(((bf16[1024,1024]{1,0:T(8,128)(2,1)}), bf16[8192,1024]{1,0:T(8,128)(2,1)}) %all-gather.5.cloned.1.call-update) | async-done | bytes 16777232 | tf_op jit(solution)/shard_map/all_gather | solution.py:24
  250.4 15.8 %fusion.18 = f32[512,8192]{1,0:T(8,128)} fusion(bf16[8192,1024]{1,0:T(8,128)(2,1)} %all-gather.5.cloned.1.call-done, bf16[1,512,1024]{2,1,0:T(8,128)(2,1)S(1)} %copy-done), kind=kOutput, calls=%fused_computation.15 | convolution fusion | flops 8589934592 | bytes 34603008 | tf_op jit(solution)/shard_map/dot_general | solution.py:27
  266.2 0.0 copy-done.2
  266.2 11.5 %fusion = bf16[1,512,8192]{2,1,0:T(8,128)(2,1)} fusion(f32[512,8192]{1,0:T(8,128)} %fusion.18, bf16[512,16]{0,1:T(8,128)(2,1)S(1)} %convolution_convert_fusion, bf16[1,16,8192]{2,1,0:T(8,128)(2,1)S(1)} %copy-done.2), kind=kOutput, calls=%fused_computation.1 | convolution fusion | flops 146800640 | bytes 25444352 | tf_op jit(solution)/shard_map/dot_general | solution.py:36
  277.7 15.5 %fusion.9 = bf16[1,512,1024]{2,1,0:T(8,128)(2,1)} fusion(f32[512,1024]{1,0:T(8,128)S(1)} %fusion.23, bf16[8192,1024]{1,0:T(8,128)(2,1)} %all-gather.5.cloned.1.call-done, bf16[1,512,8192]{2,1,0:T(8,128)(2,1)} %param.5), kind=kOutput, calls=%fused_computation.9 | convolution fusion | flops 8591507456 | bytes 28311552 | tf_op jit(solution)/shard_map/dot_general | solution.py:22
Async XLA Ops:
  7.2 1.2 copy-start
  7.2 40.6 %all-gather.3.cloned.1.call-start = ((), (), s32[]{:S(2)}) async-start(), calls=%async_computation | async-start | bytes 2621440 | tf_op jit(solution)/shard_map/all_gather | solution.py:15
  7.9 89.7 %all-reduce.3.cloned.1.call-start = ((), (), s32[]{:S(2)}) async-start(), calls=%async_computation.2 | async-start | bytes 1179648 | tf_op jit(solution)/shard_map/psum | solution.py:41
  8.4 8.2 %copy-start.1 = (bf16[1,512,8192]{2,1,0:T(8,128)(2,1)S(1)}, bf16[1,512,8192]{2,1,0:T(8,128)(2,1)}, u32[]{:S(2)}) copy-start(bf16[1,512,8192]{2,1,0:T(8,128)(2,1)} %param.5) | copy-start | bytes 25165828
  15.6 32.1 %copy-start.3 = (bf16[1,16,1024]{2,1,0:T(8,128)(2,1)S(1)}, bf16[1,16,1024]{2,1,0:T(8,128)(2,1)}, u32[]{:S(2)}) copy-start(bf16[1,16,1024]{2,1,0:T(8,128)(2,1)} %param.8) | copy-start | bytes 98308
  18.6 231.8 %all-gather.5.cloned.1.call-start = ((), (), s32[]{:S(2)}) async-start(), calls=%async_computation.1 | async-start | bytes 18874368 | tf_op jit(solution)/shard_map/all_gather | solution.py:24
  100.9 165.3 %copy-start.2 = (bf16[1,16,8192]{2,1,0:T(8,128)(2,1)S(1)}, bf16[1,16,8192]{2,1,0:T(8,128)(2,1)}, u32[]{:S(2)}) copy-start(bf16[1,16,8192]{2,1,0:T(8,128)(2,1)} %param.7) | copy-start | bytes 786436
Sparse Core Ops, SparseCore 0:
  9.8 37.8 all-gather.2
  51.3 46.2 all-reduce.2
  99.3 151.0 all-gather.4
where the time goes:
time: 300 us
  waiting for transfers between devices  228 us (76%)
  matrix products  53.4 us (18%)
  between operations  13.8 us (5%)
  other arithmetic  3.34 us (1%)
    all_gather x1, waiting for transfers between devices, body(): lax.all_gather(panel, 'blk', axis=0, tiled=True)  149 us
    psum x1, waiting for transfers between devices, body(): sum_down, sum_up = lax.psum((local_down, local_up), 'seq')  49.4 us
    all_gather x1, waiting for transfers between devices, body(): panel = lax.all_gather(base_weight, 'seq', axis=1, tiled=True)  28.9 us
    dot_general x1, matrix products, body(): lax.dot_general(output_cotangent, lax.all_gather(panel, 'blk', axis=0, ti...  15.8 us
    dot_general x1, matrix products, body(): jnp.dot(token_inputs, lax.all_gather(panel, 'blk', axis=0, tiled=True), p...  15.5 us
    dot_general x1, matrix products, body(): jnp.dot(lowrank_backward, down_matrix, preferred_element_type=jnp.float32)  11.5 us
  transfers between devices with their start and end apart: 3, of which 3 were waited for; matrix products, arithmetic and copies ran while one was open for 5% of the time, Pallas kernels for 0%

commit v1 on v0

--- a/solution.py
+++ b/solution.py
@@ -4,6 +4,19 @@
 from jax.sharding import PartitionSpec as P
 
 adapter_scale = 2.0
+
+
+def gather_around(value, axis, dim):
+    ways = lax.axis_size(axis)
+    up = [(d, (d + 1) % ways) for d in range(ways)]
+    down = [(d, (d - 1) % ways) for d in range(ways)]
+    earlier, later = ([value], [value])
+    for _ in range(ways // 2):
+        earlier.append(lax.ppermute(earlier[-1], axis, up))
+    for _ in range((ways - 1) // 2):
+        later.append(lax.ppermute(later[-1], axis, down))
+    line = jnp.concatenate([*earlier[::-1], *later[1:]], axis=dim)
+    return jnp.roll(line, (lax.axis_index(axis) - ways // 2) * value.shape[dim], axis=dim)
 
 
 def body(activations, base_weight, adapter_down, adapter_up, cotangent):
@@ -20,9 +33,7 @@
         output_cotangent, up_matrix.T, preferred_element_type=jnp.float32
     ).astype(jnp.bfloat16)
     frozen_keys = jnp.dot(
-        token_inputs,
-        lax.all_gather(panel, "blk", axis=0, tiled=True),
-        preferred_element_type=jnp.float32,
+        token_inputs, gather_around(panel, "blk", 0), preferred_element_type=jnp.float32
     )
     frozen_gradient = lax.dot_general(
         output_cotangent,

time: 300 us -> 441 us (1.47)
  the two profiles are of different devices: /device:TPU:0 before, /device:TPU:16 now
where the time goes in v1:
time: 441 us; the launch traced here: 440 us
  waiting for transfers between devices  287 us (65%)
  matrix products  57.7 us (13%)
  local copies, waits for them, and re-layouts  48 us (11%)
  starting transfers between devices  30.3 us (7%)
  between operations  13.8 us (3%)
    ppermute x4, waiting for transfers between devices, gather_around(): earlier.append(lax.ppermute(earlier[-1], axis, up))  240 us
    unnamed x32, local copies, waits for them, and re-layouts  44.9 us
    all_gather x1, waiting for transfers between devices, body(): panel = lax.all_gather(base_weight, 'seq', axis=1, tiled=True)  24.2 us
    ppermute x4, starting transfers between devices, gather_around(): earlier.append(lax.ppermute(earlier[-1], axis, up))  23.4 us
    ppermute x3, waiting for transfers between devices, gather_around(): later.append(lax.ppermute(later[-1], axis, down))  22.3 us
    dot_general x1, matrix products, body(): lax.dot_general(output_cotangent, lax.all_gather(panel, 'blk', axis=0, ti...  15.7 us
    dot_general x1, matrix products, body(): jnp.dot(token_inputs, gather_around(panel, 'blk', 0), preferred_element_t...  15.2 us
    dot_general x1, matrix products, body(): jnp.dot(lowrank_backward, down_matrix, preferred_element_type=jnp.float32)  11.5 us
  transfers between devices with their start and end apart: 10, of which 7 were waited for; matrix products, arithmetic and copies ran while one was open for 18% of the time, Pallas kernels for 0%

profile of v1, /device:TPU:16, one launch (start us, length us, event | category | flops | bytes accessed | tf_op | source)
XLA Modules:
  0.0 439.9 jit_solution(3326842346471647799)
XLA Ops:
  9.5 5.7 %fusion.18 = bf16[512,16]{0,1:T(8,128)(2,1)S(1)} fusion(bf16[1,512,8192]{2,1,0:T(8,128)(2,1)} %param.5, bf16[1,16,8192]{2,1,0:T(8,128)(2,1)} %param.7), kind=kOutput, calls=%fused_computation.12 | convolution fusion | flops 134225920 | bytes 8667136 | tf_op jit(solution)/shard_map/dot_general | solution.py:29
  16.1 5.8 %fusion.3 = f32[16,8192]{1,0:T(8,128)} fusion(bf16[512,16]{0,1:T(8,128)(2,1)S(1)} %convolution_convert_fusion, bf16[1,512,8192]{2,1,0:T(8,128)(2,1)} %param.5), kind=kOutput, calls=%fused_computation.4 | convolution fusion | flops 134217728 | bytes 8929280 | tf_op jit(solution)/shard_map/dot_general | solution.py:50
  21.9 24.2 %all-gather.3.cloned.1.call-done = bf16[1024,1024]{1,0:T(8,128)(2,1)} async-done(((bf16[1024,256]{1,0:T(8,128)(2,1)}), bf16[1024,1024]{1,0:T(8,128)(2,1)}) %all-gather.3.cloned.1.call-update) | async-done | bytes 2097168 | tf_op jit(solution)/shard_map/all_gather | solution.py:28
  46.2 25.7 %collective-permute-done = bf16[1024,1024]{1,0:T(8,128)(2,1)S(1)} collective-permute-done((bf16[1024,1024]{1,0:T(8,128)(2,1)}, bf16[1024,1024]{1,0:T(8,128)(2,1)S(1)}, u32[]{:S(2)}, u32[]{:S(2)}) %collective-permute-start) | collective-permute-done | bytes 2097184 | tf_op jit(solution)/shard_map/ppermute | solution.py:15
  73.2 1.7 collective-permute-start.4
  75.0 58.5 %collective-permute-done.1 = bf16[1024,1024]{1,0:T(8,128)(2,1)S(1)} collective-permute-done((bf16[1024,1024]{1,0:T(8,128)(2,1)S(1)}, bf16[1024,1024]{1,0:T(8,128)(2,1)S(1)}, u32[]{:S(2)}, u32[]{:S(2)}) %collective-permute-start.1) | collective-permute-done | bytes 2097184 | tf_op jit(solution)/shard_map/ppermute | solution.py:15
  134.8 10.0 %collective-permute-done.4 = bf16[1024,1024]{1,0:T(8,128)(2,1)} collective-permute-done((bf16[1024,1024]{1,0:T(8,128)(2,1)}, bf16[1024,1024]{1,0:T(8,128)(2,1)}, u32[]{:S(2)}, u32[]{:S(2)}) %collective-permute-start.4) | collective-permute-done | bytes 2097184 | tf_op jit(solution)/shard_map/ppermute | solution.py:17
  144.8 2.7 collective-permute-start.5
  147.5 124.4 %collective-permute-done.2 = bf16[1024,1024]{1,0:T(8,128)(2,1)} collective-permute-done((bf16[1024,1024]{1,0:T(8,128)(2,1)S(1)}, bf16[1024,1024]{1,0:T(8,128)(2,1)}, u32[]{:S(2)}, u32[]{:S(2)}) %collective-permute-start.2) | collective-permute-done | bytes 2097184 | tf_op jit(solution)/shard_map/ppermute | solution.py:15
  271.8 23.4 %collective-permute-start.3 = (bf16[1024,1024]{1,0:T(8,128)(2,1)}, bf16[1024,1024]{1,0:T(8,128)(2,1)}, u32[]{:S(2)}, u32[]{:S(2)}) collective-permute-start(bf16[1024,1024]{1,0:T(8,128)(2,1)} %collective-permute-done.2), channel_id=1, source_target_pairs={{0,4},{4,8},{8,12},{12,16},{16,20},{20,24},{24,28},{28,0},{1,5},{5... | collective-permute-start | bytes 6291464 | tf_op jit(solution)/shard_map/ppermute | solution.py:15
  295.2 1.8 fusion.29
  297.0 12.3 %collective-permute-done.5 = bf16[1024,1024]{1,0:T(8,128)(2,1)} collective-permute-done((bf16[1024,1024]{1,0:T(8,128)(2,1)}, bf16[1024,1024]{1,0:T(8,128)(2,1)}, u32[]{:S(2)}, u32[]{:S(2)}) %collective-permute-start.5) | collective-permute-done | bytes 2097184 | tf_op jit(solution)/shard_map/ppermute | solution.py:17
  309.3 2.3 collective-permute-start.6
  311.6 1.9 multiply_bitcast_fusion
  314.9 31.0 %collective-permute-done.3 = bf16[1024,1024]{1,0:T(8,128)(2,1)} collective-permute-done((bf16[1024,1024]{1,0:T(8,128)(2,1)}, bf16[1024,1024]{1,0:T(8,128)(2,1)}, u32[]{:S(2)}, u32[]{:S(2)}) %collective-permute-start.3) | collective-permute-done | bytes 2097184 | tf_op jit(solution)/shard_map/ppermute | solution.py:15
  346.0 3.1 constant_dynamic-update-slice_fusion.15
  349.1 3.1 constant_dynamic-update-slice_fusion.14
  352.1 3.2 constant_dynamic-update-slice_fusion.13
  355.4 3.3 constant_dynamic-update-slice_fusion.12
  358.7 1.6 constant_dynamic-update-slice_fusion.11
  360.2 3.1 constant_dynamic-update-slice_fusion.10
  363.3 3.1 constant_dynamic-update-slice_fusion.9
  366.4 3.1 constant_dynamic-update-slice_fusion.8
  369.5 3.1 constant_dynamic-update-slice_fusion.7
  372.6 3.1 constant_dynamic-update-slice_fusion.6
  378.7 1.6 constant_dynamic-update-slice_fusion.3
  380.3 3.1 constant_dynamic-update-slice_fusion.2
  383.4 3.1 constant_dynamic-update-slice_fusion.1
  386.5 3.1 constant_dynamic-update-slice_fusion
  389.5 15.2 %fusion.13 = bf16[1,512,1024]{1,2,0:T(8,128)(2,1)S(1)} fusion(f32[512,1024]{0,1:T(8,128)} %fusion.29, bf16[1,512,8192]{2,1,0:T(8,128)(2,1)} %param.5, bf16[16384,1024]{1,0:T(8,128)(2,1)} %constant_dynamic-update-slice_fusion, s32[]{:T(128)S(6)} %select_n.14), kind=kOutput, calls=%fused_computation.11 | convolution fusion | flops 8591507456 | bytes 28311556 | tf_op jit(solution)/shard_map/dot_general | solution.py:35
  406.1 15.7 %fusion.24 = f32[512,8192]{1,0:T(8,128)} fusion(bf16[8192,1024]{1,0:T(8,128)(2,1)} %all-gather.5.cloned.1.call-done, bf16[1,512,1024]{2,1,0:T(8,128)(2,1)S(1)} %copy-done), kind=kOutput, calls=%fused_computation.17 | convolution fusion | flops 8589934592 | bytes 34603008 | tf_op jit(solution)/shard_map/dot_general | solution.py:38
  421.8 11.5 %fusion.2 = bf16[1,512,8192]{2,1,0:T(8,128)(2,1)} fusion(f32[512,8192]{1,0:T(8,128)} %fusion.24, bf16[512,16]{0,1:T(8,128)(2,1)S(1)} %convolution_convert_fusion, bf16[1,16,8192]{2,1,0:T(8,128)(2,1)S(1)} %copy-done.6), kind=kOutput, calls=%fused_computation.3 | convolution fusion | flops 146800640 | bytes 25444352 | tf_op jit(solution)/shard_map/dot_general | solution.py:47
  (34 shorter events, 11.9 us)
Async XLA Ops:
  7.2 1.2 copy-start
  7.2 288.0 %copy-start.7 = (bf16[1,16,1024]{2,1,0:T(8,128)(2,1)S(1)}, bf16[1,16,1024]{2,1,0:T(8,128)(2,1)}, u32[]{:S(2)}) copy-start(bf16[1,16,1024]{2,1,0:T(8,128)(2,1)} %param.8) | copy-start | bytes 98308
  7.2 38.9 %all-gather.3.cloned.1.call-start = ((), (), s32[]{:S(2)}) async-start(), calls=%async_computation | async-start | bytes 2621440 | tf_op jit(solution)/shard_map/all_gather | solution.py:28
  7.9 303.7 %all-reduce.3.cloned.1.call-start = ((), (), s32[]{:S(2)}) async-start(), calls=%async_computation.2 | async-start | bytes 1179648 | tf_op jit(solution)/shard_map/psum | solution.py:52
  21.9 384.2 %all-gather.5.cloned.1.call-start = ((), (), s32[]{:S(2)}) async-start(), calls=%async_computation.1 | async-start | bytes 18874368 | tf_op jit(solution)/shard_map/all_gather | solution.py:40
  46.1 312.5 %copy-start.1 = (bf16[1024,1024]{1,0:T(8,128)(2,1)S(1)}, bf16[1024,1024]{1,0:T(8,128)(2,1)}, u32[]{:S(2)}) copy-start(bf16[1024,1024]{1,0:T(8,128)(2,1)} %all-gather.3.cloned.1.call-done) | copy-start | bytes 6291460
  46.1 25.7 %collective-permute-start = (bf16[1024,1024]{1,0:T(8,128)(2,1)}, bf16[1024,1024]{1,0:T(8,128)(2,1)S(1)}, u32[]{:S(2)}, u32[]{:S(2)}) collective-permute-start(bf16[1024,1024]{1,0:T(8,128)(2,1)} %all-gather.3.cloned.1.call-done), channel_id=1, source_target_pairs={{0,4},{4,8},{8,12},{12,16},{16,20},{20,24},{24,28},{28,0},{1,5},{5... | collective-permute-start | bytes 6291464 | tf_op jit(solution)/shard_map/ppermute | solution.py:15
  71.9 1.4 copy-start.2
  73.2 60.2 %collective-permute-start.1 = (bf16[1024,1024]{1,0:T(8,128)(2,1)S(1)}, bf16[1024,1024]{1,0:T(8,128)(2,1)S(1)}, u32[]{:S(2)}, u32[]{:S(2)}) collective-permute-start(bf16[1024,1024]{1,0:T(8,128)(2,1)S(1)} %collective-permute-done), channel_id=1, source_target_pairs={{0,4},{4,8},{8,12},{12,16},{16,20},{20,24},{24,28},{28,0},{1,5},{5... | collective-permute-start | bytes 6291464 | tf_op jit(solution)/shard_map/ppermute | solution.py:15
  73.2 71.6 %collective-permute-start.4 = (bf16[1024,1024]{1,0:T(8,128)(2,1)}, bf16[1024,1024]{1,0:T(8,128)(2,1)}, u32[]{:S(2)}, u32[]{:S(2)}) collective-permute-start(bf16[1024,1024]{1,0:T(8,128)(2,1)} %all-gather.3.cloned.1.call-done), channel_id=1, source_target_pairs={{0,28},{4,0},{8,4},{12,8},{16,12},{20,16},{24,20},{28,24},{1,29},{... | collective-permute-start | bytes 6291464 | tf_op jit(solution)/shard_map/ppermute | solution.py:17
  133.5 1.3 copy-start.4
  134.8 137.1 %collective-permute-start.2 = (bf16[1024,1024]{1,0:T(8,128)(2,1)S(1)}, bf16[1024,1024]{1,0:T(8,128)(2,1)}, u32[]{:S(2)}, u32[]{:S(2)}) collective-permute-start(bf16[1024,1024]{1,0:T(8,128)(2,1)S(1)} %collective-permute-done.1), channel_id=1, source_target_pairs={{0,4},{4,8},{8,12},{12,16},{16,20},{20,24},{24,28},{28,0},{1,5},{5... | collective-permute-start | bytes 6291464 | tf_op jit(solution)/shard_map/ppermute | solution.py:15
  144.8 164.5 %collective-permute-start.5 = (bf16[1024,1024]{1,0:T(8,128)(2,1)}, bf16[1024,1024]{1,0:T(8,128)(2,1)}, u32[]{:S(2)}, u32[]{:S(2)}) collective-permute-start(bf16[1024,1024]{1,0:T(8,128)(2,1)} %collective-permute-done.4), channel_id=1, source_target_pairs={{0,28},{4,0},{8,4},{12,8},{16,12},{20,16},{24,20},{28,24},{1,29},{... | collective-permute-start | bytes 6291464 | tf_op jit(solution)/shard_map/ppermute | solution.py:17
  271.8 74.1 %collective-permute-start.3 = (bf16[1024,1024]{1,0:T(8,128)(2,1)}, bf16[1024,1024]{1,0:T(8,128)(2,1)}, u32[]{:S(2)}, u32[]{:S(2)}) collective-permute-start(bf16[1024,1024]{1,0:T(8,128)(2,1)} %collective-permute-done.2), channel_id=1, source_target_pairs={{0,4},{4,8},{8,12},{12,16},{16,20},{20,24},{24,28},{28,0},{1,5},{5... | collective-permute-start | bytes 6291464 | tf_op jit(solution)/shard_map/ppermute | solution.py:15
  309.3 57.1 %collective-permute-start.6 = (bf16[1024,1024]{1,0:T(8,128)(2,1)}, bf16[1024,1024]{1,0:T(8,128)(2,1)}, u32[]{:S(2)}, u32[]{:S(2)}) collective-permute-start(bf16[1024,1024]{1,0:T(8,128)(2,1)} %collective-permute-done.5), channel_id=1, source_target_pairs={{0,28},{4,0},{8,4},{12,8},{16,12},{20,16},{24,20},{28,24},{1,29},{... | collective-permute-start | bytes 6291464 | tf_op jit(solution)/shard_map/ppermute | solution.py:17
  352.1 23.5 %copy-start.5 = (bf16[1024,1024]{1,0:T(8,128)(2,1)S(1)}, bf16[1024,1024]{1,0:T(8,128)(2,1)}, u32[]{:S(2)}) copy-start(bf16[1024,1024]{1,0:T(8,128)(2,1)} %copy-done.4) | copy-start | bytes 6291460
  355.4 21.8 %copy-start.3 = (bf16[1024,1024]{1,0:T(8,128)(2,1)S(1)}, bf16[1024,1024]{1,0:T(8,128)(2,1)}, u32[]{:S(2)}) copy-start(bf16[1024,1024]{1,0:T(8,128)(2,1)} %copy-done.2) | copy-start | bytes 6291460
  406.1 15.7 %copy-start.6 = (bf16[1,16,8192]{2,1,0:T(8,128)(2,1)S(1)}, bf16[1,16,8192]{2,1,0:T(8,128)(2,1)}, u32[]{:S(2)}) copy-start(bf16[1,16,8192]{2,1,0:T(8,128)(2,1)} %param.7) | copy-start | bytes 786436
Sparse Core Ops, SparseCore 0:
  9.8 36.2 all-gather.2
  49.7 46.2 all-reduce.2
  97.7 244.7 all-gather.4
